TPU v7x, 32 devices: a whole 2x2x4 slice. The times are simulated.
32 devices in a mesh: section: 4 (over y, x), tile: 8 (over z, core).
Axes of the slice: x: 2, y: 2, z: 4, core: 2. Of those that a mesh axis runs over, the one named last changes fastest.
Arguments:
- forcing: bfloat16 [262144, 128], P(('section', 'tile')), may hold values from -6 to 6
- w_in: bfloat16 [128, 1024], replicated, may hold values from -0.5 to 0.5
- bias_in: float32 [1024], replicated, may hold values from -3 to 3
- w_out: bfloat16 [1024, 128], replicated, may hold values from -0.1875 to 0.1875
- target_tile_index: int32 [262144, 1], P(('section', 'tile')), may hold values from 0 to 7; in each aligned block of 8192 rows (0 to 8191, 8192 to 16383, ...) at most 2048 rows name the same one
- reach_slot: int32 [262144], P(('section', 'tile')), may hold values from 0 to 63
- k_ratio: float32 [4, 512], P(None, ('section', 'tile')), may hold values from 1 to 40
- x_weight: float32 [4, 512], P(None, ('section', 'tile')), may hold values from 0.05 to 0.3
- down_link: int32 [4, 512], P(None, ('section', 'tile')), may hold values from 0 to 127
- cotangent: float32 [4, 512, 128], P(None, ('section', 'tile')), may hold values from -6 to 6
Outputs:
- discharge: float32 [4, 512, 128], P(None, ('section', 'tile'))
- grad_w_in: float32 [128, 1024], replicated
- grad_bias: float32 [1024], replicated
- grad_w_out: float32 [1024, 128], replicated
Inputs may be any that keep to these rules, and one draw needn't show every extreme that they name: `target_tile_index`: among the catchments of one device, at most 2048 name the same tile, a bound that some block reaches. `down_link`: entries of last-section reaches are not used.
All inputs are finite; a program needn't handle non-finite values.
Results may differ from a plain program's by a relative error of at most 0.0038.
Values may be sent and summed in bfloat16 or wider, within the bound.
A program may use at most 192 MiB of HBM per device.

v0:
```python
import jax
import jax.numpy as jnp
from jax import lax
from jax.sharding import PartitionSpec as P


def shifted(block, axis, distance):
    devices = range(lax.axis_size(axis))
    route = [(i - distance, i) for i in devices if i - distance in devices]
    return lax.ppermute(block, axis, route)


def coefficients(k_ratio, x_weight):
    storage = 2.0 * k_ratio * (1.0 - x_weight)
    denom = storage + 1.0
    c_now = (1.0 - 2.0 * k_ratio * x_weight) / denom
    c_prev = (1.0 + 2.0 * k_ratio * x_weight) / denom
    c_keep = (storage - 1.0) / denom
    c_side = 2.0 / denom
    return (c_now, c_prev, c_keep, c_side)


def linear_combine(first, second):
    return (first[0] * second[0], second[0] * first[1] + second[1])


def route(inflow, lateral, coefs):
    c_now, c_prev, c_keep, c_side = coefs
    before = jnp.pad(inflow[:, :, :-1], ((0, 0), (0, 0), (1, 0)))
    drive = c_now[:, :, None] * inflow + c_prev[:, :, None] * before + c_side[:, :, None] * lateral
    decay = jnp.broadcast_to(c_keep[:, :, None], drive.shape)
    _, outs = lax.associative_scan(linear_combine, (decay, drive), axis=2)
    return outs


def route_back(grad_out, coefs):
    c_now, c_prev, c_keep, c_side = coefs
    decay = jnp.broadcast_to(c_keep[:, :, None], grad_out.shape)
    _, adjoint = lax.associative_scan(linear_combine, (decay, grad_out), axis=2, reverse=True)
    after = jnp.pad(adjoint[:, :, 1:], ((0, 0), (0, 0), (0, 1)))
    grad_in = c_now[:, :, None] * adjoint + c_prev[:, :, None] * after
    grad_lat = c_side[:, :, None] * adjoint
    return (grad_in, grad_lat)


def reach_link_matrix(links, span):
    return (links[:, :, None] == jnp.arange(span, dtype=jnp.int32)[None, None, :]).astype(
        jnp.float32
    )


def pass_down(reach_outflow, links, span):
    lookup_matrix = reach_link_matrix(links, span)
    section_pieces = jnp.einsum(
        "zum,zuh->zmh", lookup_matrix, reach_outflow, precision=lax.Precision.HIGHEST
    )
    summed = lax.psum_scatter(
        section_pieces.astype(jnp.bfloat16), "tile", scatter_dimension=1, tiled=True
    ).astype(jnp.float32)
    return shifted(summed, "section", 1)


def pass_up(grad_in):
    moved = shifted(grad_in, "section", -1)
    return lax.all_gather(moved, "tile", axis=1, tiled=True)


def pick_rows(entire_network, links):
    lookup_matrix = reach_link_matrix(links, entire_network.shape[1])
    return jnp.einsum(
        "pox,pxc->poc", lookup_matrix, entire_network, precision=lax.Precision.HIGHEST
    )


def local(
    forcing,
    w_in,
    bias_in,
    w_out,
    target_tile_index,
    reach_slot,
    k_ratio,
    x_weight,
    down_link,
    cotangent,
):
    tiles = lax.axis_size("tile")
    river_sections = lax.axis_size("section")
    cells = forcing.shape[0]
    groups, reaches = k_ratio.shape
    steps_len = w_out.shape[1]
    span = tiles * reaches
    capacity = 2 * cells // tiles
    pre = jnp.dot(forcing, w_in, preferred_element_type=jnp.float32) + bias_in
    hidden = jax.nn.silu(pre).astype(jnp.bfloat16)
    runoff = (0.125 * jnp.dot(hidden, w_out, preferred_element_type=jnp.float32)).astype(
        jnp.bfloat16
    )
    target = target_tile_index[:, 0]
    onehot = (target[:, None] == jnp.arange(tiles, dtype=jnp.int32)[None, :]).astype(jnp.int32)
    rank = jnp.sum((jnp.cumsum(onehot, axis=0) - 1) * onehot, axis=1)
    position = target * capacity + rank
    send_rows = jnp.zeros((tiles * capacity, steps_len), jnp.bfloat16).at[position].set(runoff)
    send_ids = (
        jnp.full((tiles * capacity,), groups * reaches, jnp.int32).at[position].set(reach_slot)
    )
    recv_rows, recv_ids = (
        lax.all_to_all(send_rows, "tile", split_axis=0, concat_axis=0, tiled=True),
        lax.all_to_all(send_ids, "tile", split_axis=0, concat_axis=0, tiled=True),
    )
    buckets = (recv_ids[:, None] == jnp.arange(groups * reaches, dtype=jnp.int32)[None, :]).astype(
        jnp.bfloat16
    )
    lateral = lax.dot_general(
        buckets, recv_rows, (((0,), (0,)), ((), ())), preferred_element_type=jnp.float32
    )
    lateral = lateral.reshape(groups, reaches, steps_len)
    coefs = coefficients(k_ratio, x_weight)
    incoming = jnp.zeros((groups, reaches, steps_len), jnp.float32)
    for level in range(river_sections):
        discharge = route(incoming, lateral, coefs)
        if level + 1 < river_sections:
            incoming = pass_down(discharge, down_link, span)
    extra = jnp.zeros((groups, reaches, steps_len), jnp.float32)
    for level in range(river_sections):
        grad_in, grad_lateral = route_back(cotangent + extra, coefs)
        if level + 1 < river_sections:
            extra = pick_rows(pass_up(grad_in), down_link)
    flat = grad_lateral.reshape(groups * reaches, steps_len).astype(jnp.bfloat16)
    back_rows = jnp.dot(buckets, flat, preferred_element_type=jnp.float32).astype(jnp.bfloat16)
    returned = lax.all_to_all(back_rows, "tile", split_axis=0, concat_axis=0, tiled=True)
    grad_runoff = returned[position]
    grad_w_out = 0.125 * lax.dot_general(
        hidden, grad_runoff, (((0,), (0,)), ((), ())), preferred_element_type=jnp.float32
    )
    grad_hidden = 0.125 * lax.dot_general(
        grad_runoff, w_out, (((1,), (1,)), ((), ())), preferred_element_type=jnp.float32
    )
    sig = jax.nn.sigmoid(pre)
    grad_pre = grad_hidden * sig * (1.0 + pre * (1.0 - sig))
    grad_bias = jnp.sum(grad_pre, axis=0)
    grad_w_in = lax.dot_general(
        forcing,
        grad_pre.astype(jnp.bfloat16),
        (((0,), (0,)), ((), ())),
        preferred_element_type=jnp.float32,
    )
    grad_w_in, grad_bias, grad_w_out = lax.psum(
        (grad_w_in, grad_bias, grad_w_out), ("section", "tile")
    )
    return (discharge, grad_w_in, grad_bias, grad_w_out)


def solution(mesh):
    placed = (
        P(("section", "tile"), None),
        P(),
        P(),
        P(),
        P(("section", "tile"), None),
        P(("section", "tile")),
        P(None, ("section", "tile")),
        P(None, ("section", "tile")),
        P(None, ("section", "tile")),
        P(None, ("section", "tile"), None),
    )
    return jax.shard_map(
        local,
        mesh=mesh,
        in_specs=placed,
        out_specs=(P(None, ("section", "tile"), None), P(), P(), P()),
        check_vma=False,
    )
```

profile of v0, /device:TPU:0, one launch (start us, length us, event | category | flops | bytes accessed | tf_op | source)
XLA Modules:
  0.0 649.4 jit_solution(12011391910219636179)
XLA Ops:
  7.2 0.9 fusion.18
  8.1 2.4 reduce-window.6
  11.2 1.0 fusion.17
  12.2 0.8 compare_select_fusion
  13.0 31.2 %scatter_custom_fusion = s32[16384]{0:T(1024)} fusion(s32[8192]{0:T(1024)S(1)} %bitcast.132, s32[8192]{0:T(1024)} %param.15, s32[]{:T(128)} %constant.15.clone.1), kind=kCustom, calls=%fused_computation.251 | custom fusion | bytes 66048 | tf_op jit(solution)/shard_map/scatter | solution.py:105
  44.3 6.3 all-to-all-start
  50.6 1.4 slice.1239
  52.0 1.4 slice.1241
  53.3 0.7 fusion.70
  58.0 19.1 %multiply_convert_fusion = (bf16[8192,1024]{1,0:T(8,128)(2,1)}, f32[8192,1024]{1,0:T(8,128)}) fusion(f32[1024]{0:T(1024)S(1)} %copy-done.7, bf16[8192,128]{1,0:T(8,128)(2,1)S(1)} %copy-done, bf16[128,1024]{1,0:T(8,128)(2,1)S(1)} %copy-done.4), kind=kOutput, calls=%fused_computation.4 | convolution fusion | flops 2197815296 | bytes 52695040 | tf_op jit(solution)/shard_map/dot_general | solution.py:94
  77.1 9.6 %fusion.2 = bf16[8192,128]{1,0:T(8,128)(2,1)} fusion(bf16[8192,1024]{1,0:T(8,128)(2,1)} %get-tuple-element.83, bf16[1024,128]{1,0:T(8,128)(2,1)S(1)} %copy-done.5), kind=kOutput, calls=%fused_computation.10 | convolution fusion | flops 2149580800 | bytes 19136512 | tf_op jit(solution)/shard_map/dot_general | solution.py:96
  86.7 24.0 %scatter_custom_fusion.1 = bf16[16384,128]{1,0:T(8,128)(2,1)} fusion(s32[8192]{0:T(1024)S(1)} %bitcast.133, bf16[8192,128]{1,0:T(8,128)(2,1)} %fusion.2, bf16[]{:T(256)} %constant.11.clone.1), kind=kCustom, calls=%fused_computation.15 | custom fusion | bytes 4194816 | tf_op jit(solution)/shard_map/scatter | solution.py:103
  110.8 5.1 all-to-all-start.1
  123.4 0.8 pad.442
  124.2 0.8 pad.443
  125.3 1.3 collective-permute-start.3
  126.9 4.2 collective-permute-done.3
  131.1 85.7 %all_gather.9 = f32[4,128,128]{2,1,0:T(8,128)S(1)} all-gather(f32[4,16,128]{2,1,0:T(8,128)S(1)} %collective-permute-done.3), channel_id=1, replica_groups=mesh['section'=4,'tile'=8] {'tile'}, dimensions={1}, use_global_device_ids=true | all-gather | bytes 294912 | tf_op jit(solution)/shard_map/all_gather | solution.py:65
  226.5 0.8 pad.457
  227.3 0.8 pad.458
  228.3 3.1 multiply_add_fusion.13
  241.0 0.8 pad.384
  241.9 0.8 pad.383
  242.8 1.3 collective-permute-start.4
  244.1 1.1 convolution_convert_fusion.3
  245.2 3.3 collective-permute-done.4
  248.6 14.4 %all_gather.10 = f32[4,128,128]{2,1,0:T(8,128)S(1)} all-gather(f32[4,16,128]{2,1,0:T(8,128)S(1)} %collective-permute-done.4), channel_id=1, replica_groups=mesh['section'=4,'tile'=8] {'tile'}, dimensions={1}, use_global_device_ids=true | all-gather | bytes 294912 | tf_op jit(solution)/shard_map/all_gather | solution.py:65
  272.6 0.8 pad.472
  273.4 0.8 pad.473
  274.2 2.8 reduce-scatter.4.cloned.1.call-done
  277.1 0.7 convert_element_type.61
  277.8 3.5 collective-permute-start
  281.4 1.4 collective-permute-done
  288.0 1.3 collective-permute-start.5
  293.9 0.8 pad.399
  294.8 0.8 pad.398
  295.7 1.1 convolution_convert_fusion.2
  296.8 14.3 %all_gather.11 = f32[4,128,128]{2,1,0:T(8,128)S(1)} all-gather(f32[4,16,128]{2,1,0:T(8,128)S(1)} %collective-permute-done.5), channel_id=1, replica_groups=mesh['section'=4,'tile'=8] {'tile'}, dimensions={1}, use_global_device_ids=true | all-gather | bytes 294912 | tf_op jit(solution)/shard_map/all_gather | solution.py:65
  320.8 0.8 pad.488
  321.6 0.8 pad.487
  322.5 5.6 reduce-scatter.6.cloned.1.call-done
  328.1 0.7 convert_element_type.63
  328.9 3.6 collective-permute-start.1
  332.5 4.4 convolution_convert_fusion
  336.9 4.5 all-to-all-start.2
  351.2 0.8 pad.414
  352.2 0.8 pad.413
  353.0 1.1 convolution_convert_fusion.1
  354.2 33.0 %reduce-scatter.8.cloned.1.call-done = bf16[4,16,128]{2,1,0:T(8,128)(2,1)} async-done(((bf16[4,128,128]{2,1,0:T(8,128)(2,1)}), bf16[4,16,128]{2,1,0:T(8,128)(2,1)}) %reduce-scatter.8.cloned.1.call-update) | async-done | bytes 16400 | tf_op jit(solution)/shard_map/reduce_scatter | solution.py:57
  387.2 0.7 convert_element_type.65
  387.9 3.4 collective-permute-start.2
  391.3 1.6 collective-permute-done.2
  401.0 35.7 %all-to-all-done.2 = bf16[8,2048,128]{2,1,0:T(8,128)(2,1)} async-done(((bf16[8,2048,128]{2,1,0:T(8,128)(2,1)}), bf16[8,2048,128]{2,1,0:T(8,128)(2,1)}, u32[]{:S(2)}, u32[]{:S(2)}) %all-to-all-start.2) | async-done | bytes 4194336 | tf_op jit(solution)/shard_map/all_to_all | solution.py:131
  436.7 30.7 %gather_fusion = bf16[8192,128]{1,0:T(8,128)(2,1)} fusion(bf16[16384,128]{1,0:T(8,128)(2,1)} %bitcast.14, s32[8192]{0:T(1024)S(1)} %broadcast_clamp_fusion), kind=kCustom, calls=%fused_computation | custom fusion | bytes 4227072 | tf_op jit(solution)/shard_map/gather | solution.py:132
  467.4 11.8 %convolution_multiply_fusion.1 = f32[1024,128]{1,0:T(8,128)} fusion(bf16[8192,1024]{1,0:T(8,128)(2,1)} %get-tuple-element.83, bf16[8192,128]{1,0:T(8,128)(2,1)} %gather_fusion), kind=kOutput, calls=%fused_computation.20 | convolution fusion | flops 2147614720 | bytes 19398656 | tf_op jit(solution)/shard_map/dot_general | solution.py:133
  479.2 21.9 %fusion.84 = (f32[1024]{0:T(1024)S(1)}, bf16[8192,1024]{1,0:T(8,128)(2,1)}) fusion(f32[8192,1024]{1,0:T(8,128)} %get-tuple-element.84, f32[1024]{0:T(1024)S(1)} %copy-done.7, bf16[8192,128]{1,0:T(8,128)(2,1)S(1)} %copy-done.1, bf16[1024,128]{1,0:T(8,128)(2,1)S(1)} %copy-done.6), kind=kOutput, calls=%fused_computation.296 | convolution fusion | flops 2248145920 | bytes 52699136 | tf_op jit(solution)/shard_map/dot_general | solution.py:136
  501.1 8.9 %fusion.10 = f32[128,1024]{0,1:T(8,128)} fusion(bf16[8192,128]{1,0:T(8,128)(2,1)S(1)} %copy-done, bf16[8192,1024]{1,0:T(8,128)(2,1)} %get-tuple-element.87), kind=kOutput, calls=%fused_computation.19 | convolution fusion | flops 2147483648 | bytes 19398656 | tf_op jit(solution)/shard_map/dot_general | solution.py:142
  511.9 0.8 pad.429
  512.9 0.8 pad.428
  513.7 0.6 add.906
  514.3 37.1 %psum.22 = f32[1024]{0:T(1024)} all-reduce(f32[1024]{0:T(1024)S(1)} %get-tuple-element.86), channel_id=1, replica_groups=mesh['section'=4,'tile'=8] {'section','tile'}, use_global_device_ids=true, to_apply=%region_10.11 | all-reduce | flops 1024 | bytes 8192 | tf_op jit(solution)/shard_map/psum | solution.py:148
  551.4 87.2 %all-reduce.122.cloned.1.call-done = (f32[128,1024]{0,1:T(8,128)}, f32[1024,128]{1,0:T(8,128)}) async-done(((f32[128,1024]{0,1:T(8,128)}, f32[1024,128]{1,0:T(8,128)}), (f32[128,1024]{0,1:T(8,128)}, f32[1024,128]{1,0:T(8,128)})) %all-reduce.122.cloned.1.call-update) | async-done | bytes 1048592 | tf_op jit(solution)/shard_map/psum | solution.py:148
  638.6 2.0 copy.99
  640.6 1.9 copy.104
  (508 shorter events, 80.0 us)
Async XLA Ops:
  7.2 50.8 %copy-start = (bf16[8192,128]{1,0:T(8,128)(2,1)S(1)}, bf16[8192,128]{1,0:T(8,128)(2,1)}, u32[]{:S(2)}) copy-start(bf16[8192,128]{1,0:T(8,128)(2,1)} %param.10) | copy-start | bytes 6291460
  7.2 50.8 %copy-start.4 = (bf16[128,1024]{1,0:T(8,128)(2,1)S(1)}, bf16[128,1024]{1,0:T(8,128)(2,1)}, u32[]{:S(2)}) copy-start(bf16[128,1024]{1,0:T(8,128)(2,1)} %param.11) | copy-start | bytes 786436
  7.2 50.8 %copy-start.7 = (f32[1024]{0:T(1024)S(1)}, f32[1024]{0:T(1024)}, u32[]{:S(2)}) copy-start(f32[1024]{0:T(1024)} %param.12) | copy-start | bytes 12292
  44.3 66.5 %all-to-all-start = ((s32[8,2048,1]{1,2,0:T(1,128)}), s32[8,2048,1]{1,2,0:T(1,128)S(1)}, u32[]{:S(2)}, u32[]{:S(2)}) async-start(s32[8,2048,1]{1,2,0:T(1,128)} %bitcast.5), calls=%async_computation | async-start | bytes 131072 | tf_op jit(solution)/shard_map/all_to_all | solution.py:109
  58.0 19.1 %copy-start.5 = (bf16[1024,128]{1,0:T(8,128)(2,1)S(1)}, bf16[1024,128]{1,0:T(8,128)(2,1)}, u32[]{:S(2)}) copy-start(bf16[1024,128]{1,0:T(8,128)(2,1)} %param.13) | copy-start | bytes 786436
  110.8 7.2 %copy-start.2 = (f32[4,16,128]{2,1,0:T(8,128)S(1)}, f32[4,16,128]{2,1,0:T(8,128)}, u32[]{:S(2)}) copy-start(f32[4,16,128]{2,1,0:T(8,128)} %param.19) | copy-start | bytes 98308
  110.8 117.5 %all-to-all-start.1 = ((bf16[8,2048,128]{2,1,0:T(8,128)(2,1)}), bf16[8,2048,128]{2,1,0:T(8,128)(2,1)}, u32[]{:S(2)}, u32[]{:S(2)}) async-start(bf16[8,2048,128]{2,1,0:T(8,128)(2,1)} %bitcast.89), calls=%async_computation.1 | async-start | bytes 8388608 | tf_op jit(solution)/shard_map/all_to_all | solution.py:108
  115.9 100.9 %copy-start.3 = (s32[4,16]{1,0:T(4,128)S(1)}, s32[4,16]{1,0:T(4,128)}, u32[]{:S(2)}) copy-start(s32[4,16]{1,0:T(4,128)} %param.18) | copy-start | bytes 772
  115.9 161.2 %reduce-scatter.4.cloned.1.call-start = ((), (), s32[]{:S(2)}) async-start(), calls=%async_computation.6 | async-start | bytes 147456 | tf_op jit(solution)/shard_map/reduce_scatter | solution.py:57
  125.3 5.8 collective-permute-start.3
  242.8 5.8 collective-permute-start.4
  245.2 82.9 %reduce-scatter.6.cloned.1.call-start = ((), (), s32[]{:S(2)}) async-start(), calls=%async_computation.7 | async-start | bytes 147456 | tf_op jit(solution)/shard_map/reduce_scatter | solution.py:57
  277.8 5.1 collective-permute-start
  288.0 8.8 %collective-permute-start.5 = (f32[4,16,128]{2,1,0:T(8,128)S(1)}, f32[4,16,128]{2,1,0:T(8,128)S(1)}, u32[]{:S(2)}, u32[]{:S(2)}) collective-permute-start(f32[4,16,128]{2,1,0:T(8,128)S(1)} %get-tuple-element.69), channel_id=1, source_target_pairs={{8,0},{16,8},{24,16},{9,1},{17,9},{25,17},{10,2},{18,10},{26,18},{... | collective-permute-start | bytes 98312 | tf_op jit(solution)/shard_map/ppermute | solution.py:10
  328.9 12.6 %collective-permute-start.1 = (f32[4,16,128]{2,1,0:T(8,128)S(1)}, f32[4,16,128]{2,1,0:T(8,128)S(1)}, u32[]{:S(2)}, u32[]{:S(2)}) collective-permute-start(f32[4,16,128]{2,1,0:T(8,128)S(1)} %convert_element_type.63), channel_id=1, source_target_pairs={{0,8},{8,16},{16,24},{1,9},{9,17},{17,25},{2,10},{10,18},{18,26},{... | collective-permute-start | bytes 98312 | tf_op jit(solution)/shard_map/ppermute | solution.py:10
  336.9 99.8 %all-to-all-start.2 = ((bf16[8,2048,128]{2,1,0:T(8,128)(2,1)}), bf16[8,2048,128]{2,1,0:T(8,128)(2,1)}, u32[]{:S(2)}, u32[]{:S(2)}) async-start(bf16[8,2048,128]{2,1,0:T(8,128)(2,1)} %bitcast.88), calls=%async_computation.5 | async-start | bytes 8388608 | tf_op jit(solution)/shard_map/all_to_all | solution.py:131
  341.4 45.8 %reduce-scatter.8.cloned.1.call-start = ((), (), s32[]{:S(2)}) async-start(), calls=%async_computation.8 | async-start | bytes 147456 | tf_op jit(solution)/shard_map/reduce_scatter | solution.py:57
  354.2 284.4 %all-reduce.122.cloned.1.call-start = ((), (), s32[]{:S(2)}) async-start(), calls=%async_computation.9 | async-start | bytes 2097152 | tf_op jit(solution)/shard_map/psum | solution.py:148
  387.9 4.9 collective-permute-start.2
  467.4 11.8 %copy-start.1 = (bf16[8192,128]{1,0:T(8,128)(2,1)S(1)}, bf16[8192,128]{1,0:T(8,128)(2,1)}, u32[]{:S(2)}) copy-start(bf16[8192,128]{1,0:T(8,128)(2,1)} %gather_fusion) | copy-start | bytes 6291460
  467.4 11.8 %copy-start.6 = (bf16[1024,128]{1,0:T(8,128)(2,1)S(1)}, bf16[1024,128]{1,0:T(8,128)(2,1)}, u32[]{:S(2)}) copy-start(bf16[1024,128]{1,0:T(8,128)(2,1)} %param.13) | copy-start | bytes 786436
Sparse Core Ops, SparseCore 0:
  245.3 31.6 reduce-scatter.3
  296.9 31.1 reduce-scatter.5
  354.3 32.8 reduce-scatter.7
  510.2 128.3 all-reduce.121
where the time goes:
time: 660 us; the launch traced here: 649 us
  waiting for transfers between devices  175 us (27%)
  local copies, waits for them, and re-layouts  173 us (26%)
  blocking collectives  152 us (23%)
  matrix products  82.9 us (13%)
  starting transfers between devices  30.8 us (5%)
  other arithmetic  19.5 us (3%)
  between operations  16.7 us (3%)
    all_gather x3, blocking collectives, pass_up(): return lax.all_gather(moved, 'tile', axis=1, tiled=True)  114 us
    psum x1, waiting for transfers between devices, local(): lax.psum((grad_w_in, grad_bias, grad_w_out), ('section', 'tile'))  87.2 us
    reduce_scatter x3, waiting for transfers between devices, pass_down(): lax.psum_scatter(section_pieces.astype(jnp.bfloat16), 'tile', scatter_dim...  41.4 us
    psum x1, blocking collectives, local(): lax.psum((grad_w_in, grad_bias, grad_w_out), ('section', 'tile'))  37.1 us
    all_to_all x1, waiting for transfers between devices, local(): lax.all_to_all(back_rows, 'tile', split_axis=0, concat_axis=0, tiled=True)  35.7 us
    scatter x1, local copies, waits for them, and re-layouts, local(): jnp.full((tiles * capacity,), groups * reaches, jnp.int32).at[position]  31.2 us
    gather x1, local copies, waits for them, and re-layouts, local(): grad_runoff = returned[position]  30.7 us
    scatter x1, local copies, waits for them, and re-layouts, local(): jnp.zeros((tiles * capacity, steps_len), jnp.bfloat16).at[position]  24 us
  transfers between devices with their start and end apart: 13, of which 9 were waited for; matrix products, arithmetic and copies ran while one was open for 22% of the time, Pallas kernels for 0%

commit v1 on v0

--- a/solution.py
+++ b/solution.py
@@ -2,6 +2,27 @@
 import jax.numpy as jnp
 from jax import lax
 from jax.sharding import PartitionSpec as P
+
+
+def collect(x, axis, dim):
+    size, index, rows = (lax.axis_size(axis), lax.axis_index(axis), x.shape[dim])
+    right = [(i, (i + 1) % size) for i in range(size)]
+    behind = [(i, (i - 1) % size) for i in range(size)]
+    whole = jnp.zeros((*x.shape[:dim], size * rows, *x.shape[dim + 1 :]), x.dtype)
+    whole = lax.dynamic_update_slice_in_dim(whole, x, index * rows, axis=dim)
+    from_left = from_right = x
+    half = size // 2
+    for step in range(1, half + 1):
+        from_left = lax.ppermute(from_left, axis, right)
+        whole = lax.dynamic_update_slice_in_dim(
+            whole, from_left, (index - step) % size * rows, axis=dim
+        )
+        if step < size - half:
+            from_right = lax.ppermute(from_right, axis, behind)
+            whole = lax.dynamic_update_slice_in_dim(
+                whole, from_right, (index + step) % size * rows, axis=dim
+            )
+    return whole
 
 
 def shifted(block, axis, distance):
@@ -62,7 +83,7 @@
 
 def pass_up(grad_in):
     moved = shifted(grad_in, "section", -1)
-    return lax.all_gather(moved, "tile", axis=1, tiled=True)
+    return collect(moved, "tile", 1)
 
 
 def pick_rows(entire_network, links):

time: 660 us -> 672 us (1.018)
  blocking collectives: 152 us -> 38 us
  waiting for transfers between devices: 175 us -> 251 us
  starting transfers between devices: 30.8 us -> 76.5 us
    all_gather x3 -> x0, blocking collectives: 114 us -> none  [pass_up(): return lax.all_gather(moved, 'tile', axis=1, tiled=True)]
    ppermute x0 -> x21, waiting for transfers between devices: none -> 81.8 us  [the longest x12 81.2 us: collect(): from_left = lax.ppermute(from_left, axis, right)]
    ppermute x0 -> x21, starting transfers between devices: none -> 44.8 us  [the longest x9 29.7 us: collect(): from_right = lax.ppermute(from_right, axis, behind)]
  transfers between devices with their start and end apart: 13 -> 34, of which waited for: 9 -> 21; matrix products, arithmetic and copies ran while one was open for 22% -> 22% of each run, Pallas kernels for 0% -> 0%
where the time goes in v1:
time: 672 us; the launch traced here: 661 us
  waiting for transfers between devices  251 us (37%)
  local copies, waits for them, and re-layouts  174 us (26%)
  matrix products  85 us (13%)
  starting transfers between devices  76.5 us (11%)
  blocking collectives  38 us (6%)
  other arithmetic  19.5 us (3%)
  between operations  16.8 us (2%)
    psum x1, waiting for transfers between devices, local(): lax.psum((grad_w_in, grad_bias, grad_w_out), ('section', 'tile'))  87.6 us
    ppermute x12, waiting for transfers between devices, collect(): from_left = lax.ppermute(from_left, axis, right)  81.2 us
    reduce_scatter x3, waiting for transfers between devices, pass_down(): lax.psum_scatter(section_pieces.astype(jnp.bfloat16), 'tile', scatter_dim...  38.9 us
    psum x1, blocking collectives, local(): lax.psum((grad_w_in, grad_bias, grad_w_out), ('section', 'tile'))  38 us
    all_to_all x1, waiting for transfers between devices, local(): lax.all_to_all(back_rows, 'tile', split_axis=0, concat_axis=0, tiled=True)  34.4 us
    scatter x1, local copies, waits for them, and re-layouts, local(): jnp.full((tiles * capacity,), groups * reaches, jnp.int32).at[position]  31.2 us
    gather x1, local copies, waits for them, and re-layouts, local(): grad_runoff = returned[position]  30.7 us
    ppermute x9, starting transfers between devices, collect(): from_right = lax.ppermute(from_right, axis, behind)  29.7 us
  transfers between devices with their start and end apart: 34, of which 21 were waited for; matrix products, arithmetic and copies ran while one was open for 22% of the time, Pallas kernels for 0%

profile of v1, /device:TPU:0, one launch (start us, length us, event | category | flops | bytes accessed | tf_op | source)
XLA Modules:
  0.0 661.2 jit_solution(3662277187224734019)
XLA Ops:
  7.2 0.9 fusion.18
  8.1 2.4 reduce-window.6
  11.2 1.0 fusion.17
  12.2 0.8 compare_select_fusion
  13.0 31.2 %scatter_custom_fusion = s32[16384]{0:T(1024)} fusion(s32[8192]{0:T(1024)S(1)} %bitcast.132, s32[8192]{0:T(1024)} %param.15, s32[]{:T(128)} %constant.105.clone.1), kind=kCustom, calls=%fused_computation.251 | custom fusion | bytes 66048 | tf_op jit(solution)/shard_map/scatter | solution.py:126
  44.3 6.3 all-to-all-start
  50.6 1.4 slice.1239
  52.0 1.4 slice.1241
  61.4 19.1 %multiply_convert_fusion = (bf16[8192,1024]{1,0:T(8,128)(2,1)}, f32[8192,1024]{1,0:T(8,128)}) fusion(f32[1024]{0:T(1024)S(1)} %copy-done.6, bf16[8192,128]{1,0:T(8,128)(2,1)S(1)} %copy-done, bf16[128,1024]{1,0:T(8,128)(2,1)S(1)} %copy-done.4), kind=kOutput, calls=%fused_computation.4 | convolution fusion | flops 2197815296 | bytes 52695040 | tf_op jit(solution)/shard_map/dot_general | solution.py:115
  80.5 11.6 %fusion.2 = bf16[8192,128]{1,0:T(8,128)(2,1)} fusion(bf16[8192,1024]{1,0:T(8,128)(2,1)} %get-tuple-element.83, bf16[1024,128]{1,0:T(8,128)(2,1)} %param.13), kind=kOutput, calls=%fused_computation.10 | convolution fusion | flops 2149580800 | bytes 19136512 | tf_op jit(solution)/shard_map/dot_general | solution.py:117
  92.2 24.2 %scatter_custom_fusion.1 = bf16[16384,128]{1,0:T(8,128)(2,1)} fusion(s32[8192]{0:T(1024)S(1)} %bitcast.133, bf16[8192,128]{1,0:T(8,128)(2,1)} %fusion.2, bf16[]{:T(256)} %constant.111.clone.1), kind=kCustom, calls=%fused_computation.15 | custom fusion | bytes 4194816 | tf_op jit(solution)/shard_map/scatter | solution.py:124
  116.4 5.1 all-to-all-start.1
  126.1 0.8 pad.443
  127.2 1.3 collective-permute-start.3
  128.9 4.1 collective-permute-done.3
  133.0 3.5 collective-permute-start.5
  136.6 57.8 %collective-permute-done.4 = f32[4,16,128]{2,1,0:T(8,128)S(1)} collective-permute-done((f32[4,16,128]{2,1,0:T(8,128)S(1)}, f32[4,16,128]{2,1,0:T(8,128)S(1)}, u32[]{:S(2)}, u32[]{:S(2)}) %collective-permute-start.4) | collective-permute-done | bytes 32800 | tf_op jit(solution)/shard_map/ppermute | solution.py:16
  194.3 3.5 collective-permute-start.7
  197.9 1.7 collective-permute-done.6
  199.6 3.5 collective-permute-start.9
  203.1 1.7 collective-permute-done.8
  204.8 12.7 %collective-permute-start.10 = (f32[4,16,128]{2,1,0:T(8,128)S(1)}, f32[4,16,128]{2,1,0:T(8,128)S(1)}, u32[]{:S(2)}, u32[]{:S(2)}) collective-permute-start(f32[4,16,128]{2,1,0:T(8,128)S(1)} %collective-permute-done.8), channel_id=1, source_target_pairs={{0,1},{1,2},{2,3},{3,4},{4,5},{5,6},{6,7},{7,0},{8,9},{9,10},{10,1... | collective-permute-start | bytes 98312 | tf_op jit(solution)/shard_map/ppermute | solution.py:16
  229.2 0.8 pad.458
  230.2 3.1 multiply_add_fusion.13
  243.0 1.3 collective-permute-start.11
  246.0 1.1 convolution_convert_fusion.3
  247.2 1.6 collective-permute-done.11
  248.8 1.5 collective-permute-start.12
  250.3 2.0 collective-permute-start.13
  252.4 1.6 collective-permute-done.12
  253.9 0.8 collective-permute-start.14
  254.8 2.7 collective-permute-start.15
  257.5 1.5 collective-permute-done.14
  259.1 3.5 collective-permute-start.17
  262.7 1.5 collective-permute-done.16
  264.3 5.1 collective-permute-done.18
  280.6 4.6 reduce-scatter.4.cloned.1.call-done
  286.0 3.4 collective-permute-start
  289.6 1.4 collective-permute-done
  296.2 1.3 collective-permute-start.19
  303.9 1.1 convolution_convert_fusion.2
  305.1 3.5 collective-permute-start.21
  308.7 1.7 collective-permute-done.20
  310.4 3.6 collective-permute-start.23
  314.0 1.6 collective-permute-done.22
  315.6 3.6 collective-permute-start.25
  319.2 1.6 collective-permute-done.24
  320.8 5.1 collective-permute-done.26
  338.1 4.8 collective-permute-start.1
  343.0 4.4 convolution_convert_fusion
  347.3 4.6 all-to-all-start.2
  363.5 1.1 convolution_convert_fusion.1
  364.7 34.3 %reduce-scatter.8.cloned.1.call-done = bf16[4,16,128]{2,1,0:T(8,128)(2,1)} async-done(((bf16[4,128,128]{2,1,0:T(8,128)(2,1)}), bf16[4,16,128]{2,1,0:T(8,128)(2,1)}) %reduce-scatter.8.cloned.1.call-update) | async-done | bytes 16400 | tf_op jit(solution)/shard_map/reduce_scatter | solution.py:78
  399.7 3.4 collective-permute-start.2
  403.1 1.6 collective-permute-done.2
  412.8 34.4 %all-to-all-done.2 = bf16[8,2048,128]{2,1,0:T(8,128)(2,1)} async-done(((bf16[8,2048,128]{2,1,0:T(8,128)(2,1)}), bf16[8,2048,128]{2,1,0:T(8,128)(2,1)}, u32[]{:S(2)}, u32[]{:S(2)}) %all-to-all-start.2) | async-done | bytes 4194336 | tf_op jit(solution)/shard_map/all_to_all | solution.py:152
  447.2 30.7 %gather_fusion = bf16[8192,128]{1,0:T(8,128)(2,1)} fusion(bf16[16384,128]{1,0:T(8,128)(2,1)} %bitcast.14, s32[8192]{0:T(1024)S(1)} %broadcast_clamp_fusion), kind=kCustom, calls=%fused_computation | custom fusion | bytes 4227072 | tf_op jit(solution)/shard_map/gather | solution.py:153
  477.9 11.8 %convolution_multiply_fusion.1 = f32[1024,128]{1,0:T(8,128)} fusion(bf16[8192,1024]{1,0:T(8,128)(2,1)} %get-tuple-element.83, bf16[8192,128]{1,0:T(8,128)(2,1)} %gather_fusion), kind=kOutput, calls=%fused_computation.20 | convolution fusion | flops 2147614720 | bytes 19398656 | tf_op jit(solution)/shard_map/dot_general | solution.py:154
  489.7 21.9 %fusion.84 = (f32[1024]{0:T(1024)S(1)}, bf16[8192,1024]{1,0:T(8,128)(2,1)}) fusion(f32[8192,1024]{1,0:T(8,128)} %get-tuple-element.84, f32[1024]{0:T(1024)S(1)} %copy-done.6, bf16[8192,128]{1,0:T(8,128)(2,1)S(1)} %copy-done.1, bf16[1024,128]{1,0:T(8,128)(2,1)S(1)} %copy-done.5), kind=kOutput, calls=%fused_computation.320 | convolution fusion | flops 2248145920 | bytes 52699136 | tf_op jit(solution)/shard_map/dot_general | solution.py:157
  511.6 8.9 %fusion.10 = f32[128,1024]{0,1:T(8,128)} fusion(bf16[8192,128]{1,0:T(8,128)(2,1)S(1)} %copy-done, bf16[8192,1024]{1,0:T(8,128)(2,1)} %get-tuple-element.87), kind=kOutput, calls=%fused_computation.19 | convolution fusion | flops 2147483648 | bytes 19398656 | tf_op jit(solution)/shard_map/dot_general | solution.py:163
  524.8 38.0 %psum.22 = f32[1024]{0:T(1024)} all-reduce(f32[1024]{0:T(1024)S(1)} %get-tuple-element.86), channel_id=1, replica_groups=mesh['section'=4,'tile'=8] {'section','tile'}, use_global_device_ids=true, to_apply=%region_10.11 | all-reduce | flops 1024 | bytes 8192 | tf_op jit(solution)/shard_map/psum | solution.py:169
  562.8 87.6 %all-reduce.122.cloned.1.call-done = (f32[128,1024]{0,1:T(8,128)}, f32[1024,128]{1,0:T(8,128)}) async-done(((f32[128,1024]{0,1:T(8,128)}, f32[1024,128]{1,0:T(8,128)}), (f32[128,1024]{0,1:T(8,128)}, f32[1024,128]{1,0:T(8,128)})) %all-reduce.122.cloned.1.call-update) | async-done | bytes 1048592 | tf_op jit(solution)/shard_map/psum | solution.py:169
  650.4 2.0 copy.99
  652.5 1.9 copy.225
  (572 shorter events, 96.1 us)
Async XLA Ops:
  7.2 54.2 %copy-start = (bf16[8192,128]{1,0:T(8,128)(2,1)S(1)}, bf16[8192,128]{1,0:T(8,128)(2,1)}, u32[]{:S(2)}) copy-start(bf16[8192,128]{1,0:T(8,128)(2,1)} %param.10) | copy-start | bytes 6291460
  7.2 52.6 %copy-start.2 = (f32[4,16,128]{2,1,0:T(8,128)S(1)}, f32[4,16,128]{2,1,0:T(8,128)}, u32[]{:S(2)}) copy-start(f32[4,16,128]{2,1,0:T(8,128)} %param.19) | copy-start | bytes 98308
  7.2 54.2 %copy-start.4 = (bf16[128,1024]{1,0:T(8,128)(2,1)S(1)}, bf16[128,1024]{1,0:T(8,128)(2,1)}, u32[]{:S(2)}) copy-start(bf16[128,1024]{1,0:T(8,128)(2,1)} %param.11) | copy-start | bytes 786436
  7.2 54.2 %copy-start.6 = (f32[1024]{0:T(1024)S(1)}, f32[1024]{0:T(1024)}, u32[]{:S(2)}) copy-start(f32[1024]{0:T(1024)} %param.12) | copy-start | bytes 12292
  44.3 72.1 %all-to-all-start = ((s32[8,2048,1]{1,2,0:T(1,128)}), s32[8,2048,1]{1,2,0:T(1,128)S(1)}, u32[]{:S(2)}, u32[]{:S(2)}) async-start(s32[8,2048,1]{1,2,0:T(1,128)} %bitcast.5), calls=%async_computation | async-start | bytes 131072 | tf_op jit(solution)/shard_map/all_to_all | solution.py:130
  116.4 102.0 %copy-start.3 = (s32[4,16]{1,0:T(4,128)S(1)}, s32[4,16]{1,0:T(4,128)}, u32[]{:S(2)}) copy-start(s32[4,16]{1,0:T(4,128)} %param.18) | copy-start | bytes 772
  116.4 113.8 %all-to-all-start.1 = ((bf16[8,2048,128]{2,1,0:T(8,128)(2,1)}), bf16[8,2048,128]{2,1,0:T(8,128)(2,1)}, u32[]{:S(2)}, u32[]{:S(2)}) async-start(bf16[8,2048,128]{2,1,0:T(8,128)(2,1)} %bitcast.89), calls=%async_computation.1 | async-start | bytes 8388608 | tf_op jit(solution)/shard_map/all_to_all | solution.py:129
  121.5 163.7 %reduce-scatter.4.cloned.1.call-start = ((), (), s32[]{:S(2)}) async-start(), calls=%async_computation.6 | async-start | bytes 147456 | tf_op jit(solution)/shard_map/reduce_scatter | solution.py:78
  127.2 5.8 collective-permute-start.3
  133.0 61.4 %collective-permute-start.4 = (f32[4,16,128]{2,1,0:T(8,128)S(1)}, f32[4,16,128]{2,1,0:T(8,128)S(1)}, u32[]{:S(2)}, u32[]{:S(2)}) collective-permute-start(f32[4,16,128]{2,1,0:T(8,128)S(1)} %collective-permute-done.3), channel_id=1, source_target_pairs={{0,1},{1,2},{2,3},{3,4},{4,5},{5,6},{6,7},{7,0},{8,9},{9,10},{10,1... | collective-permute-start | bytes 98312 | tf_op jit(solution)/shard_map/ppermute | solution.py:16
  133.0 61.4 %collective-permute-start.5 = (f32[4,16,128]{2,1,0:T(8,128)S(1)}, f32[4,16,128]{2,1,0:T(8,128)S(1)}, u32[]{:S(2)}, u32[]{:S(2)}) collective-permute-start(f32[4,16,128]{2,1,0:T(8,128)S(1)} %collective-permute-done.3), channel_id=1, source_target_pairs={{0,7},{1,0},{2,1},{3,2},{4,3},{5,4},{6,5},{7,6},{8,15},{9,8},{10,9... | collective-permute-start | bytes 98312 | tf_op jit(solution)/shard_map/ppermute | solution.py:21
  194.3 5.2 collective-permute-start.6
  194.3 5.2 collective-permute-start.7
  199.6 5.2 collective-permute-start.8
  199.6 18.4 %collective-permute-start.9 = (f32[4,16,128]{2,1,0:T(8,128)S(1)}, f32[4,16,128]{2,1,0:T(8,128)S(1)}, u32[]{:S(2)}, u32[]{:S(2)}) collective-permute-start(f32[4,16,128]{2,1,0:T(8,128)S(1)} %collective-permute-done.7), channel_id=1, source_target_pairs={{0,7},{1,0},{2,1},{3,2},{4,3},{5,4},{6,5},{7,6},{8,15},{9,8},{10,9... | collective-permute-start | bytes 98312 | tf_op jit(solution)/shard_map/ppermute | solution.py:21
  204.8 13.6 %collective-permute-start.10 = (f32[4,16,128]{2,1,0:T(8,128)S(1)}, f32[4,16,128]{2,1,0:T(8,128)S(1)}, u32[]{:S(2)}, u32[]{:S(2)}) collective-permute-start(f32[4,16,128]{2,1,0:T(8,128)S(1)} %collective-permute-done.8), channel_id=1, source_target_pairs={{0,1},{1,2},{2,3},{3,4},{4,5},{5,6},{6,7},{7,0},{8,9},{9,10},{10,1... | collective-permute-start | bytes 98312 | tf_op jit(solution)/shard_map/ppermute | solution.py:16
  243.0 5.8 collective-permute-start.11
  247.1 90.3 %reduce-scatter.6.cloned.1.call-start = ((), (), s32[]{:S(2)}) async-start(), calls=%async_computation.7 | async-start | bytes 147456 | tf_op jit(solution)/shard_map/reduce_scatter | solution.py:78
  248.8 5.1 collective-permute-start.12
  250.3 4.5 collective-permute-start.13
  253.9 5.1 collective-permute-start.14
  254.8 4.3 collective-permute-start.15
  259.1 5.1 collective-permute-start.16
  259.1 5.1 collective-permute-start.17
  264.2 5.1 collective-permute-start.18
  286.0 5.0 collective-permute-start
  296.2 8.9 %collective-permute-start.19 = (f32[4,16,128]{2,1,0:T(8,128)S(1)}, f32[4,16,128]{2,1,0:T(8,128)S(1)}, u32[]{:S(2)}, u32[]{:S(2)}) collective-permute-start(f32[4,16,128]{2,1,0:T(8,128)S(1)} %get-tuple-element.69), channel_id=1, source_target_pairs={{8,0},{16,8},{24,16},{9,1},{17,9},{25,17},{10,2},{18,10},{26,18},{... | collective-permute-start | bytes 98312 | tf_op jit(solution)/shard_map/ppermute | solution.py:31
  305.1 5.3 collective-permute-start.20
  305.1 5.2 collective-permute-start.21
  310.4 5.2 collective-permute-start.22
  310.4 5.2 collective-permute-start.23
  315.6 5.2 collective-permute-start.24
  315.6 5.2 collective-permute-start.25
  320.8 5.2 collective-permute-start.26
  338.1 13.9 %collective-permute-start.1 = (f32[4,16,128]{2,1,0:T(8,128)S(1)}, f32[4,16,128]{2,1,0:T(8,128)S(1)}, u32[]{:S(2)}, u32[]{:S(2)}) collective-permute-start(f32[4,16,128]{2,1,0:T(8,128)S(1)} %convert_element_type.63), channel_id=1, source_target_pairs={{0,8},{8,16},{16,24},{1,9},{9,17},{17,25},{2,10},{10,18},{18,26},{... | collective-permute-start | bytes 98312 | tf_op jit(solution)/shard_map/ppermute | solution.py:31
  347.3 99.8 %all-to-all-start.2 = ((bf16[8,2048,128]{2,1,0:T(8,128)(2,1)}), bf16[8,2048,128]{2,1,0:T(8,128)(2,1)}, u32[]{:S(2)}, u32[]{:S(2)}) async-start(bf16[8,2048,128]{2,1,0:T(8,128)(2,1)} %bitcast.88), calls=%async_computation.5 | async-start | bytes 8388608 | tf_op jit(solution)/shard_map/all_to_all | solution.py:152
  351.9 47.0 %reduce-scatter.8.cloned.1.call-start = ((), (), s32[]{:S(2)}) async-start(), calls=%async_computation.8 | async-start | bytes 147456 | tf_op jit(solution)/shard_map/reduce_scatter | solution.py:78
  364.7 285.8 %all-reduce.122.cloned.1.call-start = ((), (), s32[]{:S(2)}) async-start(), calls=%async_computation.9 | async-start | bytes 2097152 | tf_op jit(solution)/shard_map/psum | solution.py:169
  399.7 5.0 collective-permute-start.2
  477.9 11.8 %copy-start.1 = (bf16[8192,128]{1,0:T(8,128)(2,1)S(1)}, bf16[8192,128]{1,0:T(8,128)(2,1)}, u32[]{:S(2)}) copy-start(bf16[8192,128]{1,0:T(8,128)(2,1)} %gather_fusion) | copy-start | bytes 6291460
  477.9 11.8 %copy-start.5 = (bf16[1024,128]{1,0:T(8,128)(2,1)S(1)}, bf16[1024,128]{1,0:T(8,128)(2,1)}, u32[]{:S(2)}) copy-start(bf16[1024,128]{1,0:T(8,128)(2,1)} %param.13) | copy-start | bytes 786436
Sparse Core Ops, SparseCore 0:
  247.3 37.9 reduce-scatter.3
  305.2 31.2 reduce-scatter.5
  364.8 34.1 reduce-scatter.7
  520.6 129.7 all-reduce.121
